TPU v7x, 32 devices: a whole 2x2x4 slice. The times are simulated.
32 devices in a mesh: rep: 16 (over z, x, core), shard: 2 (over y).
Axes of the slice: x: 2, y: 2, z: 4, core: 2. Of those that a mesh axis runs over, the one named last changes fastest.
Arguments:
- images: bfloat16 [160, 197, 768], P(('rep', 'shard')), may hold values from -6 to 6
- ln1_gain: bfloat16 [768], P('shard'), may hold values from 0.25 to 1.75
- first_norm_bias: bfloat16 [768], P('shard'), may hold values from -3 to 3
- qkv_weight: bfloat16 [768, 2304], P('shard'), may hold values from -0.21875 to 0.21875
- q_bias: bfloat16 [768], P('shard'), may hold values from -3 to 3
- v_bias: bfloat16 [768], P('shard'), may hold values from -3 to 3
- out_weight: bfloat16 [768, 768], P('shard'), may hold values from -1.75 to 1.75
- out_bias: bfloat16 [768], P('shard'), may hold values from -3 to 3
- ln2_gain: bfloat16 [768], P('shard'), may hold values from 0.25 to 1.75
- second_norm_bias: bfloat16 [768], P('shard'), may hold values from -3 to 3
- up_weight: bfloat16 [768, 3072], P('shard'), may hold values from -0.21875 to 0.21875
- up_bias: bfloat16 [3072], P('shard'), may hold values from -3 to 3
- down_weight: bfloat16 [3072, 768], P('shard'), may hold values from -0.109375 to 0.109375
- down_bias: bfloat16 [768], P('shard'), may hold values from -3 to 3
- cotangent: bfloat16 [160, 197, 768], P(('rep', 'shard')), may hold values from -6 to 6
Outputs:
- result: bfloat16 [160, 197, 768], P(('rep', 'shard'))
- grad_images: bfloat16 [160, 197, 768], P(('rep', 'shard'))
- grad_ln1_gain: float32 [768], P('shard')
- grad_ln1_bias: float32 [768], P('shard')
- grad_qkv_weight: float32 [768, 2304], P('shard')
- grad_q_bias: float32 [768], P('shard')
- grad_v_bias: float32 [768], P('shard')
- grad_out_weight: float32 [768, 768], P('shard')
- grad_out_bias: float32 [768], P('shard')
- grad_ln2_gain: float32 [768], P('shard')
- grad_ln2_bias: float32 [768], P('shard')
- grad_up_weight: float32 [768, 3072], P('shard')
- grad_up_bias: float32 [3072], P('shard')
- grad_down_weight: float32 [3072, 768], P('shard')
- grad_down_bias: float32 [768], P('shard')
All inputs are finite; a program needn't handle non-finite values.
Results may differ from a plain program's by a relative error of at most 0.012.
Values may be sent and summed in bfloat16 or wider, within the bound.
No kernel may reach another device: no remote copies, remote signals or barrier semaphores. Data moves between devices by JAX's collectives and lax.ppermute only.
A program may use at most 256 MiB of HBM per device.

v0:
```python
import jax
import jax.numpy as jnp
from jax import lax
from jax.sharding import PartitionSpec as P

HEADS = 12


def matmul(left, right):
    return jnp.dot(left, right, preferred_element_type=jnp.float32)


def norm_statistics(token_rows):
    row_average = jnp.mean(token_rows, axis=-1, keepdims=True)
    centred = token_rows - row_average
    var = jnp.mean(centred * centred, axis=-1, keepdims=True)
    scale_factor = lax.rsqrt(var + 1e-06)
    return (centred * scale_factor, scale_factor)


def norm_backward(normalized_gradient, standardized_input, scale_factor, norm_gain):
    scaled_rows = normalized_gradient * norm_gain
    return scale_factor * (
        scaled_rows
        - jnp.mean(scaled_rows, axis=-1, keepdims=True)
        - standardized_input * jnp.mean(scaled_rows * standardized_input, axis=-1, keepdims=True)
    )


def gelu_parts(pre):
    cdf = 0.5 * (1.0 + lax.erf(pre * 0.7071067811865476))
    dens = jnp.exp(-0.5 * pre * pre) * 0.3989422804014327
    return (pre * cdf, cdf + pre * dens)


def per_device(
    images,
    ln1_gain,
    first_norm_bias,
    qkv_weight,
    q_bias,
    v_bias,
    out_weight,
    out_bias,
    ln2_gain,
    second_norm_bias,
    up_weight,
    up_bias,
    down_weight,
    down_bias,
    cotangent,
):
    count, seq, width = images.shape
    heads = HEADS
    head = width // heads
    scale = head ** (-0.5)
    single_float = jnp.float32
    brain_float16 = jnp.bfloat16
    attention_complete = (
        lax.all_gather(ln1_gain, "shard", axis=0, tiled=True),
        lax.all_gather(first_norm_bias, "shard", axis=0, tiled=True),
        lax.all_gather(qkv_weight, "shard", axis=0, tiled=True),
        lax.all_gather(q_bias, "shard", axis=0, tiled=True),
        lax.all_gather(v_bias, "shard", axis=0, tiled=True),
        lax.all_gather(out_weight, "shard", axis=0, tiled=True),
        lax.all_gather(out_bias, "shard", axis=0, tiled=True),
    )
    first_norm_gain = attention_complete[0].astype(single_float)
    token_rows = images.reshape(-1, width).astype(single_float)
    first_standardized, first_scale_factor = norm_statistics(token_rows)
    first_normalized = (
        first_standardized * first_norm_gain + attention_complete[1].astype(single_float)
    ).astype(brain_float16)
    bias_all = jnp.concatenate(
        [
            attention_complete[3].astype(single_float),
            jnp.zeros((width,), single_float),
            attention_complete[4].astype(single_float),
        ]
    )
    qkv = (matmul(first_normalized, attention_complete[2]) + bias_all).astype(brain_float16)
    query = qkv[:, :width].reshape(count, seq, heads, head)
    keys = qkv[:, width : 2 * width].reshape(count, seq, heads, head)
    values = qkv[:, 2 * width :].reshape(count, seq, heads, head)
    scores = jnp.einsum("nqhe,nkhe->nhqk", query, keys, preferred_element_type=single_float) * scale
    top = jnp.max(scores, axis=-1, keepdims=True)
    total = jnp.sum(jnp.exp(scores - top), axis=-1, keepdims=True)
    lse = top + jnp.log(total)
    prob_b = jnp.exp(scores - lse).astype(brain_float16)
    context = (
        jnp.einsum("nhqk,nkhe->nqhe", prob_b, values, preferred_element_type=single_float)
        .astype(brain_float16)
        .reshape(-1, width)
    )
    hidden_activation = (
        token_rows
        + matmul(context, attention_complete[5])
        + attention_complete[6].astype(single_float)
    )
    perceptron_complete = (
        lax.all_gather(ln2_gain, "shard", axis=0, tiled=True),
        lax.all_gather(second_norm_bias, "shard", axis=0, tiled=True),
        lax.all_gather(up_weight, "shard", axis=0, tiled=True),
        lax.all_gather(up_bias, "shard", axis=0, tiled=True),
        lax.all_gather(down_weight, "shard", axis=0, tiled=True),
        lax.all_gather(down_bias, "shard", axis=0, tiled=True),
    )
    second_norm_gain = perceptron_complete[0].astype(single_float)
    second_standardized, second_scale_factor = norm_statistics(hidden_activation)
    second_normalized = (
        second_standardized * second_norm_gain + perceptron_complete[1].astype(single_float)
    ).astype(brain_float16)
    pre = matmul(second_normalized, perceptron_complete[2]) + perceptron_complete[3].astype(
        single_float
    )
    act, slope = gelu_parts(pre)
    act_b = act.astype(brain_float16)
    result = (
        hidden_activation
        + matmul(act_b, perceptron_complete[4])
        + perceptron_complete[5].astype(single_float)
    ).astype(brain_float16)
    perceptron_backward = (
        lax.all_gather(ln2_gain, "shard", axis=0, tiled=True),
        lax.all_gather(second_norm_bias, "shard", axis=0, tiled=True),
        lax.all_gather(up_weight, "shard", axis=0, tiled=True),
        lax.all_gather(up_bias, "shard", axis=0, tiled=True),
        lax.all_gather(down_weight, "shard", axis=0, tiled=True),
        lax.all_gather(down_bias, "shard", axis=0, tiled=True),
    )
    cot = cotangent.reshape(-1, width)
    cotangent_float32 = cot.astype(single_float)
    g_down_bias = jnp.sum(cotangent_float32, axis=0)
    g_down = matmul(act_b.T, cot)
    dpre = matmul(cot, perceptron_backward[4].T) * slope
    dpre_b = dpre.astype(brain_float16)
    g_up_bias = jnp.sum(dpre, axis=0)
    g_up = matmul(second_normalized.T, dpre_b)
    second_normalized_gradient = matmul(dpre_b, perceptron_backward[2].T)
    second_norm_gain_gradient = jnp.sum(second_normalized_gradient * second_standardized, axis=0)
    g_ln2_bias = jnp.sum(second_normalized_gradient, axis=0)
    middle_gradient = cotangent_float32 + norm_backward(
        second_normalized_gradient,
        second_standardized,
        second_scale_factor,
        perceptron_backward[0].astype(single_float),
    )
    mlp_grads = (second_norm_gain_gradient, g_ln2_bias, g_up, g_up_bias, g_down, g_down_bias)
    mlp_pieces = (
        lax.psum_scatter(
            mlp_grads[0].astype(jnp.bfloat16), "shard", scatter_dimension=0, tiled=True
        ).astype(jnp.float32),
        lax.psum_scatter(
            mlp_grads[1].astype(jnp.bfloat16), "shard", scatter_dimension=0, tiled=True
        ).astype(jnp.float32),
        lax.psum_scatter(
            mlp_grads[2].astype(jnp.bfloat16), "shard", scatter_dimension=0, tiled=True
        ).astype(jnp.float32),
        lax.psum_scatter(
            mlp_grads[3].astype(jnp.bfloat16), "shard", scatter_dimension=0, tiled=True
        ).astype(jnp.float32),
        lax.psum_scatter(
            mlp_grads[4].astype(jnp.bfloat16), "shard", scatter_dimension=0, tiled=True
        ).astype(jnp.float32),
        lax.psum_scatter(
            mlp_grads[5].astype(jnp.bfloat16), "shard", scatter_dimension=0, tiled=True
        ).astype(jnp.float32),
    )
    p_ln2_gain, p_ln2_bias, p_up, p_up_bias, p_down, p_down_bias = mlp_pieces
    attention_backward = (
        lax.all_gather(ln1_gain, "shard", axis=0, tiled=True),
        lax.all_gather(first_norm_bias, "shard", axis=0, tiled=True),
        lax.all_gather(qkv_weight, "shard", axis=0, tiled=True),
        lax.all_gather(q_bias, "shard", axis=0, tiled=True),
        lax.all_gather(v_bias, "shard", axis=0, tiled=True),
        lax.all_gather(out_weight, "shard", axis=0, tiled=True),
        lax.all_gather(out_bias, "shard", axis=0, tiled=True),
    )
    dmiddle_b = middle_gradient.astype(brain_float16)
    g_out_bias = jnp.sum(middle_gradient, axis=0)
    g_out = matmul(context.T, dmiddle_b)
    dcontext = (
        matmul(dmiddle_b, attention_backward[5].T)
        .astype(brain_float16)
        .reshape(count, seq, heads, head)
    )
    again = jnp.einsum("nqhe,nkhe->nhqk", query, keys, preferred_element_type=single_float) * scale
    prob = jnp.exp(again - lse)
    prob_again = prob.astype(brain_float16)
    dprob = jnp.einsum("nqhe,nkhe->nhqk", dcontext, values, preferred_element_type=single_float)
    dvalue = jnp.einsum(
        "nhqk,nqhe->nkhe", prob_again, dcontext, preferred_element_type=single_float
    ).reshape(-1, width)
    delta = jnp.sum(prob * dprob, axis=-1, keepdims=True)
    dscore = (prob * (dprob - delta) * scale).astype(brain_float16)
    dquery = jnp.einsum(
        "nhqk,nkhe->nqhe", dscore, keys, preferred_element_type=single_float
    ).reshape(-1, width)
    dkey = jnp.einsum(
        "nhqk,nqhe->nkhe", dscore, query, preferred_element_type=single_float
    ).reshape(-1, width)
    g_q_bias = jnp.sum(dquery, axis=0)
    g_v_bias = jnp.sum(dvalue, axis=0)
    dqkv = jnp.concatenate([dquery, dkey, dvalue], axis=1).astype(brain_float16)
    g_qkv = matmul(first_normalized.T, dqkv)
    first_normalized_gradient = matmul(dqkv, attention_backward[2].T)
    first_norm_gain_gradient = jnp.sum(first_normalized_gradient * first_standardized, axis=0)
    g_ln1_bias = jnp.sum(first_normalized_gradient, axis=0)
    input_gradient = (
        middle_gradient
        + norm_backward(
            first_normalized_gradient,
            first_standardized,
            first_scale_factor,
            attention_backward[0].astype(single_float),
        )
    ).astype(brain_float16)
    attn_grads = (
        first_norm_gain_gradient,
        g_ln1_bias,
        g_qkv,
        g_q_bias,
        g_v_bias,
        g_out,
        g_out_bias,
    )
    attn_pieces = (
        lax.psum_scatter(
            attn_grads[0].astype(jnp.bfloat16), "shard", scatter_dimension=0, tiled=True
        ).astype(jnp.float32),
        lax.psum_scatter(
            attn_grads[1].astype(jnp.bfloat16), "shard", scatter_dimension=0, tiled=True
        ).astype(jnp.float32),
        lax.psum_scatter(
            attn_grads[2].astype(jnp.bfloat16), "shard", scatter_dimension=0, tiled=True
        ).astype(jnp.float32),
        lax.psum_scatter(
            attn_grads[3].astype(jnp.bfloat16), "shard", scatter_dimension=0, tiled=True
        ).astype(jnp.float32),
        lax.psum_scatter(
            attn_grads[4].astype(jnp.bfloat16), "shard", scatter_dimension=0, tiled=True
        ).astype(jnp.float32),
        lax.psum_scatter(
            attn_grads[5].astype(jnp.bfloat16), "shard", scatter_dimension=0, tiled=True
        ).astype(jnp.float32),
        lax.psum_scatter(
            attn_grads[6].astype(jnp.bfloat16), "shard", scatter_dimension=0, tiled=True
        ).astype(jnp.float32),
    )
    p_ln1_gain, p_ln1_bias, p_qkv, p_q_bias, p_v_bias, p_out, p_out_bias = attn_pieces
    (
        p_ln1_gain,
        p_ln1_bias,
        p_qkv,
        p_q_bias,
        p_v_bias,
        p_out,
        p_out_bias,
        p_ln2_gain,
        p_ln2_bias,
        p_up,
        p_up_bias,
        p_down,
        p_down_bias,
    ) = lax.psum(
        (
            p_ln1_gain,
            p_ln1_bias,
            p_qkv,
            p_q_bias,
            p_v_bias,
            p_out,
            p_out_bias,
            p_ln2_gain,
            p_ln2_bias,
            p_up,
            p_up_bias,
            p_down,
            p_down_bias,
        ),
        "rep",
    )
    return (
        result.reshape(count, seq, width),
        input_gradient.reshape(count, seq, width),
        p_ln1_gain,
        p_ln1_bias,
        p_qkv,
        p_q_bias,
        p_v_bias,
        p_out,
        p_out_bias,
        p_ln2_gain,
        p_ln2_bias,
        p_up,
        p_up_bias,
        p_down,
        p_down_bias,
    )


def solution(mesh):
    in_specs = (
        P(("rep", "shard"), None, None),
        P("shard"),
        P("shard"),
        P("shard", None),
        P("shard"),
        P("shard"),
        P("shard", None),
        P("shard"),
        P("shard"),
        P("shard"),
        P("shard", None),
        P("shard"),
        P("shard", None),
        P("shard"),
        P(("rep", "shard"), None, None),
    )
    out_specs = (
        P(("rep", "shard"), None, None),
        P(("rep", "shard"), None, None),
        P("shard"),
        P("shard"),
        P("shard", None),
        P("shard"),
        P("shard"),
        P("shard", None),
        P("shard"),
        P("shard"),
        P("shard"),
        P("shard", None),
        P("shard"),
        P("shard", None),
        P("shard"),
    )
    return jax.shard_map(
        per_device, mesh=mesh, in_specs=in_specs, out_specs=out_specs, check_vma=False
    )
```

profile of v0, /device:TPU:1, one launch (start us, length us, event | category | flops | bytes accessed | tf_op | source)
XLA Modules:
  0.0 828.6 jit_solution(5341018697626411092)
XLA Ops:
  13.1 3.9 all-gather
  17.1 3.2 all-gather.1
  20.4 3.5 all-gather.2
  24.0 3.8 all-gather.3
  27.8 3.7 all-gather.4
  32.1 3.7 all-gather.5
  35.9 3.7 all-gather.6
  40.2 4.0 all-gather.7
  47.8 13.3 %all-gather.14.cloned.1.call-done = bf16[768,2304]{1,0:T(8,128)(2,1)} async-done(((bf16[384,2304]{1,0:T(8,128)(2,1)}), bf16[768,2304]{1,0:T(8,128)(2,1)}) %all-gather.14.cloned.1.call-update) | async-done | bytes 3538960 | tf_op jit(solution)/shard_map/all_gather | solution.py:62
  61.1 6.3 add_convert_fusion
  68.8 5.8 reshape.201
  74.6 6.0 copy.66
  80.6 4.4 reshape.200
  85.0 6.0 copy.65
  91.0 4.4 reshape.199
  95.4 5.5 copy.67
  100.9 4.1 multiply_reduce_fusion.1
  112.0 3.2 copy.69
  115.1 4.6 reshape.154
  119.8 4.4 fusion.45
  126.4 23.3 %all-gather.18.cloned.1.call-done = bf16[768,3072]{1,0:T(8,128)(2,1)} async-done(((bf16[384,3072]{1,0:T(8,128)(2,1)}), bf16[768,3072]{1,0:T(8,128)(2,1)}) %all-gather.18.cloned.1.call-update) | async-done | bytes 4718608 | tf_op jit(solution)/shard_map/all_gather | solution.py:103
  149.7 13.7 %multiply_convert_fusion.1 = (bf16[985,3072]{1,0:T(8,128)(2,1)}, f32[985,3072]{1,0:T(8,128)}) fusion(f32[3072]{0:T(1024)S(1)} %bitcast.46, bf16[768,3072]{1,0:T(8,128)(2,1)} %all-gather.18.cloned.1.call-done, f32[985,768]{1,0:T(8,128)} %copy-done.5, f32[768]{0:T(1024)S(1)} %copy-done.25, f32[768]{0:T(1024)S(1)} %reshape.186, f32[985]{0:T(1024)S(1)} %add_rsqrt_fusion.1, ...), kind=kOutput, calls=%fused_computation.12 | convolution fusion | flops 4669751296 | bytes 25926344 | tf_op jit(solution)/shard_map/dot_general | solution.py:10
  163.3 50.4 %all-gather.20.cloned.1.call-done = bf16[3072,768]{1,0:T(8,128)(2,1)} async-done(((bf16[1536,768]{1,0:T(8,128)(2,1)}), bf16[3072,768]{1,0:T(8,128)(2,1)}) %all-gather.20.cloned.1.call-update) | async-done | bytes 4718608 | tf_op jit(solution)/shard_map/all_gather | solution.py:105
  213.7 11.6 %fusion.48 = (bf16[3072]{0:T(1024)(128)(2,1)S(1)}, bf16[985,3072]{1,0:T(8,128)(2,1)S(1)}) fusion(f32[985,3072]{1,0:T(8,128)} %get-tuple-element.55, f32[3072]{0:T(1024)S(1)} %bitcast.47, bf16[985,768]{1,0:T(8,128)(2,1)S(1)} %copy-done.15, bf16[3072,768]{1,0:T(8,128)(2,1)} %all-gather.20.cloned.1.call-done), kind=kOutput, calls=%fused_computation.97 | convolution fusion | flops 4684121088 | bytes 24405504 | tf_op jit(solution)/shard_map/dot_general | solution.py:10
  225.3 5.5 multiply_reduce_fusion.3
  236.3 3.6 convolution_convert_fusion.3
  239.9 4.4 reshape.202
  244.3 6.2 copy.71
  250.5 9.5 %bitcast_convert_fusion = (bf16[5,197,12,64]{1,3,2,0:T(8,128)(2,1)S(1)}, f32[5,12,64,197]{3,2,1,0:T(8,128)}) fusion(bf16[5,197,12,64]{1,3,2,0:T(8,128)(2,1)} %copy.71, f32[5,12,197,197]{2,3,1,0:T(8,128)} %copy-done, f32[5,12,197]{2,1,0:T(8,128)S(1)} %copy-done.20), kind=kOutput, calls=%fused_computation.27 | convolution fusion | flops 305795232 | bytes 15413280 | tf_op jit(solution)/shard_map/nhqk,nqhe->nkhe/dot_general | solution.py:191
  260.0 6.2 fusion.49
  266.3 3.2 copy.81
  269.4 5.7 reshape.160
  275.1 20.7 %bitcast_convert_fusion.1 = (bf16[5,197,12,64]{1,3,2,0:T(8,128)(2,1)}, f32[5,12,64,197]{3,2,1,0:T(8,128)}) fusion(bf16[5,197,12,64]{1,3,2,0:T(8,128)(2,1)S(1)} %copy-done.4, f32[5,12,197,197]{2,3,1,0:T(8,128)} %fusion.49, f32[5,12,197,197]{2,3,1,0:T(8,128)} %copy-done, f32[5,12,197]{2,1,0:T(8,128)S(1)} %copy-done.20), kind=kOutput, calls=%fused_computation.29 | convolution fusion | flops 319778464 | bytes 24727440 | tf_op jit(solution)/shard_map/nhqk,nkhe->nqhe/dot_general | solution.py:196
  295.8 4.7 copy.75
  300.4 6.1 reshape.158
  306.6 19.3 %convert_bitcast_fusion = bf16[5,197,12,64]{1,3,2,0:T(8,128)(2,1)} fusion(bf16[5,197,12,64]{1,3,2,0:T(8,128)(2,1)S(1)} %copy-done.3, f32[5,12,197,197]{2,3,1,0:T(8,128)} %fusion.49, f32[5,12,197,197]{2,3,1,0:T(8,128)} %copy-done, f32[5,12,197]{2,1,0:T(8,128)S(1)} %copy-done.20), kind=kOutput, calls=%fused_computation.49 | convolution fusion | flops 319778464 | bytes 21701520 | tf_op jit(solution)/shard_map/nhqk,nqhe->nkhe/dot_general | solution.py:199
  325.9 3.0 copy.78
  328.9 3.5 reshape.159
  337.1 6.1 convolution_convert_fusion.2
  344.5 9.7 %convolution_convert_fusion = bf16[3072,768]{1,0:T(8,128)(2,1)} fusion(bf16[985,3072]{1,0:T(8,128)(2,1)} %get-tuple-element.54, bf16[985,768]{1,0:T(8,128)(2,1)S(1)} %copy-done.16), kind=kOutput, calls=%fused_computation.23 | convolution fusion | flops 4650172416 | bytes 12283392 | tf_op jit(solution)/shard_map/dot_general | solution.py:10
  356.1 9.8 %convolution_convert_fusion.1 = bf16[768,3072]{1,0:T(8,128)(2,1)} fusion(bf16[985,3072]{1,0:T(8,128)(2,1)} %copy-done.37, f32[985,768]{1,0:T(8,128)S(1)} %copy-done.7, f32[768]{0:T(1024)S(1)} %copy-done.25, f32[768]{0:T(1024)S(1)} %reshape.186, f32[985]{0:T(1024)S(1)} %add_rsqrt_fusion.1, f32[985]{0:T(1024)S(1)} %broadcast_multiply_fusion.5), kind=kOutput, calls=%fused_computation.24 | convolution fusion | flops 4653955072 | bytes 13810376 | tf_op jit(solution)/shard_map/dot_general | solution.py:10
  368.4 3.8 all-gather.8
  374.0 10.1 %add_convert_fusion.2 = bf16[985,768]{1,0:T(8,128)(2,1)} fusion(f32[985,768]{1,0:T(8,128)S(1)} %copy-done.7, bf16[985,3072]{1,0:T(8,128)(2,1)} %get-tuple-element.54, bf16[3072,768]{1,0:T(8,128)(2,1)} %all-gather.20.cloned.1.call-done, f32[768]{0:T(1024)S(1)} %reshape.189), kind=kOutput, calls=%fused_computation.40 | convolution fusion | flops 4650083328 | bytes 15312384 | tf_op jit(solution)/shard_map/dot_general | solution.py:10
  392.3 8.6 %multiply_reduce_fusion.4 = (bf16[768]{0:T(1024)(128)(2,1)S(1)}, f32[985]{0:T(1024)S(1)}, f32[985]{0:T(1024)S(1)}, bf16[768]{0:T(1024)(128)(2,1)S(1)}, f32[985,768]{1,0:T(8,128)S(1)}) fusion(f32[985,768]{1,0:T(8,128)S(1)} %copy-done.12, f32[985]{0:T(1024)S(1)} %rsqrt.20, f32[985]{0:T(1024)S(1)} %div.27, f32[768]{0:T(1024)S(1)} %reshape.181, ...), kind=kOutput, calls=%fused_computation.32 | convolution fusion | flops 3492664576 | bytes 14151568 | tf_op jit(solution)/shard_map/dot_general | solution.py:10
  406.0 6.8 all-reduce.10
  413.5 40.4 %reduce-scatter.11.cloned.1.call-done = bf16[1536,768]{1,0:T(8,128)(2,1)} async-done(((bf16[3072,768]{1,0:T(8,128)(2,1)}), bf16[1536,768]{1,0:T(8,128)(2,1)}) %reduce-scatter.11.cloned.1.call-update) | async-done | bytes 2359312 | tf_op jit(solution)/shard_map/reduce_scatter | solution.py:162
  453.9 63.0 %reduce-scatter.9.cloned.1.call-done = bf16[384,3072]{1,0:T(8,128)(2,1)} async-done(((bf16[768,3072]{1,0:T(8,128)(2,1)}), bf16[384,3072]{1,0:T(8,128)(2,1)}) %reduce-scatter.9.cloned.1.call-update) | async-done | bytes 2359312 | tf_op jit(solution)/shard_map/reduce_scatter | solution.py:156
  516.9 304.7 %all-reduce.12 = (f32[384]{0:T(512)}, f32[384]{0:T(512)}, f32[384,2304]{1,0:T(8,128)}, f32[384]{0:T(512)}, f32[384]{0:T(512)}, /*index=5*/f32[384,768]{1,0:T(8,1...) all-reduce(f32[384]{0:T(512)S(1)} %dynamic-slice_convert_fusion.8, ...), channel_id=1, replica_groups=mesh['rep'=16,'shard'=2] {'rep'}, use_global_device_ids=true, to_apply=%region_13.0 | all-reduce | flops 3543552 | bytes 21270528 | tf_op jit(solution)/shard_map/psum | solution.py:265
  (164 shorter events, 51.6 us)
Async XLA Ops:
  7.2 53.9 %all-gather.14.cloned.1.call-start = ((), (), s32[]{:S(2)}) async-start(), calls=%async_computation.4 | async-start | bytes 5308416 | tf_op jit(solution)/shard_map/all_gather | solution.py:62
  7.9 2.1 copy-start.2
  7.9 111.9 %all-gather.16.cloned.1.call-start = ((), (), s32[]{:S(2)}) async-start(), calls=%async_computation.5 | async-start | bytes 1769472 | tf_op jit(solution)/shard_map/all_gather | solution.py:65
  8.7 141.0 %all-gather.18.cloned.1.call-start = ((), (), s32[]{:S(2)}) async-start(), calls=%async_computation.6 | async-start | bytes 7077888 | tf_op jit(solution)/shard_map/all_gather | solution.py:103
  9.4 204.3 %all-gather.20.cloned.1.call-start = ((), (), s32[]{:S(2)}) async-start(), calls=%async_computation.7 | async-start | bytes 7077888 | tf_op jit(solution)/shard_map/all_gather | solution.py:105
  10.0 403.6 %reduce-scatter.7.cloned.1.call-start = ((), (), s32[]{:S(2)}) async-start(), calls=%async_computation.9 | async-start | bytes 1769472 | tf_op jit(solution)/shard_map/reduce_scatter | solution.py:243
  10.4 2.7 copy-start.27
  10.4 6.7 copy-start.28
  10.4 9.9 %copy-start.29 = (bf16[384]{0:T(512)(128)(2,1)S(1)}, bf16[384]{0:T(512)(128)(2,1)}, u32[]{:S(2)}) copy-start(bf16[384]{0:T(512)(128)(2,1)} %param.19) | copy-start | bytes 2308
  10.4 13.5 %copy-start.30 = (bf16[384]{0:T(512)(128)(2,1)S(1)}, bf16[384]{0:T(512)(128)(2,1)}, u32[]{:S(2)}) copy-start(bf16[384]{0:T(512)(128)(2,1)} %param.20) | copy-start | bytes 2308
  10.5 17.4 %copy-start.31 = (bf16[384]{0:T(512)(128)(2,1)S(1)}, bf16[384]{0:T(512)(128)(2,1)}, u32[]{:S(2)}) copy-start(bf16[384]{0:T(512)(128)(2,1)} %param.22) | copy-start | bytes 2308
  10.5 21.7 %copy-start.32 = (bf16[384]{0:T(512)(128)(2,1)S(1)}, bf16[384]{0:T(512)(128)(2,1)}, u32[]{:S(2)}) copy-start(bf16[384]{0:T(512)(128)(2,1)} %param.23) | copy-start | bytes 2308
  10.5 25.4 %copy-start.33 = (bf16[384]{0:T(512)(128)(2,1)S(1)}, bf16[384]{0:T(512)(128)(2,1)}, u32[]{:S(2)}) copy-start(bf16[384]{0:T(512)(128)(2,1)} %param.24) | copy-start | bytes 2308
  10.5 29.7 %copy-start.26 = (bf16[1536]{0:T(1024)(128)(2,1)S(1)}, bf16[1536]{0:T(1024)(128)(2,1)}, u32[]{:S(2)}) copy-start(bf16[1536]{0:T(1024)(128)(2,1)} %param.26) | copy-start | bytes 9220
  13.1 48.0 %copy-start.10 = (f32[985,768]{1,0:T(8,128)S(1)}, f32[985,768]{1,0:T(8,128)}, u32[]{:S(2)}) copy-start(f32[985,768]{1,0:T(8,128)} %reshape.162) | copy-start | bytes 9077764
  20.3 47.1 %copy-start.23 = (f32[768]{0:T(1024)}, f32[768]{0:T(1024)S(1)}, u32[]{:S(2)}) copy-start(f32[768]{0:T(1024)S(1)} %reshape.182) | copy-start | bytes 9220
  105.0 4.5 copy-start
  109.5 2.5 copy-start.19
  119.8 4.4 copy-start.17
  124.2 1.6 copy-start.5
  124.2 25.4 %copy-start.22 = (f32[2,1,1536]{2,1,0:T(1,128)S(1)}, f32[2,1,1536]{2,1,0:T(1,128)}, u32[]{:S(2)}) copy-start(f32[2,1,1536]{2,1,0:T(1,128)} %convert_element_type.226) | copy-start | bytes 36868
  124.2 25.4 %copy-start.25 = (f32[768]{0:T(1024)S(1)}, f32[768]{0:T(1024)}, u32[]{:S(2)}) copy-start(f32[768]{0:T(1024)} %reshape.187) | copy-start | bytes 9220
  149.7 64.1 %copy-start.15 = (bf16[985,768]{1,0:T(8,128)(2,1)S(1)}, bf16[985,768]{1,0:T(8,128)(2,1)}, u32[]{:S(2)}) copy-start(bf16[985,768]{1,0:T(8,128)(2,1)} %reshape.156) | copy-start | bytes 4538884
  213.7 11.6 %copy-start.6 = (f32[985,768]{1,0:T(8,128)S(1)}, f32[985,768]{1,0:T(8,128)}, u32[]{:S(2)}) copy-start(f32[985,768]{1,0:T(8,128)} %copy-done.5) | copy-start | bytes 9077764
  213.7 11.6 %copy-start.35 = (bf16[768,3072]{1,0:T(8,128)(2,1)S(1)}, bf16[768,3072]{1,0:T(8,128)(2,1)}, u32[]{:S(2)}) copy-start(bf16[768,3072]{1,0:T(8,128)(2,1)} %all-gather.18.cloned.1.call-done) | copy-start | bytes 14155780
  225.3 5.5 copy-start.37
  230.9 3.0 copy-start.18
  232.2 1.6 copy-start.8
  236.3 177.3 %reduce-scatter.5.cloned.1.call-start = ((), (), s32[]{:S(2)}) async-start(), calls=%async_computation.8 | async-start | bytes 5308416 | tf_op jit(solution)/shard_map/reduce_scatter | solution.py:234
  244.3 6.2 copy-start.20
  250.5 9.5 %copy-start.1 = (bf16[5,197,12,64]{1,3,2,0:T(8,128)(2,1)S(1)}, bf16[5,197,12,64]{1,3,2,0:T(8,128)(2,1)}, u32[]{:S(2)}) copy-start(bf16[5,197,12,64]{1,3,2,0:T(8,128)(2,1)} %copy.71) | copy-start | bytes 4538884
  269.4 5.7 copy-start.4
  300.4 6.1 copy-start.3
  332.4 1.9 copy-start.14
  332.4 2.4 copy-start.13
  334.3 2.8 copy-start.11
  334.3 2.8 copy-start.24
  334.9 2.2 copy-start.21
  343.1 1.4 copy-start.16
  343.1 110.8 %reduce-scatter.11.cloned.1.call-start = ((), (), s32[]{:S(2)}) async-start(), calls=%async_computation.11 | async-start | bytes 7077888 | tf_op jit(solution)/shard_map/reduce_scatter | solution.py:162
  354.2 1.9 copy-start.7
  354.2 162.7 %reduce-scatter.9.cloned.1.call-start = ((), (), s32[]{:S(2)}) async-start(), calls=%async_computation.10 | async-start | bytes 7077888 | tf_op jit(solution)/shard_map/reduce_scatter | solution.py:156
  365.9 0.7 copy-start.36
  365.9 2.5 copy-start.34
  387.0 5.3 copy-start.12
  392.3 8.7 %copy-start.9 = (f32[985,768]{1,0:T(8,128)S(1)}, f32[985,768]{1,0:T(8,128)}, u32[]{:S(2)}) copy-start(f32[985,768]{1,0:T(8,128)} %copy-done.8) | copy-start | bytes 9077764
Sparse Core Ops, SparseCore 0:
  9.5 51.5 all-gather.13
  62.6 22.7 all-gather.15
  87.0 62.6 all-gather.17
  151.1 62.6 all-gather.19
  236.4 21.8 reduce-scatter.6
  343.2 47.7 reduce-scatter.4
  393.3 60.5 reduce-scatter.10
  456.8 60.0 reduce-scatter.8
where the time goes:
time: 832 us; the launch traced here: 829 us
  blocking collectives  345 us (41%)
  waiting for transfers between devices  193 us (23%)
  matrix products  154 us (19%)
  local copies, waits for them, and re-layouts  104 us (12%)
  between operations  16.2 us (2%)
  other arithmetic  16 us (2%)
    psum x1, blocking collectives, per_device(): lax.psum((p_ln1_gain, p_ln1_bias, p_qkv, p_q_bias, p_v_bias, p_out, p_out...  305 us
    dot_general x12, matrix products, matmul(): return jnp.dot(left, right, preferred_element_type=jnp.float32)  91.7 us
    reduce_scatter x1, waiting for transfers between devices, per_device(): lax.psum_scatter(mlp_grads[2].astype(jnp.bfloat16), 'shard', scatter_dime...  63 us
    all_gather x1, waiting for transfers between devices, per_device(): lax.all_gather(down_weight, 'shard', axis=0, tiled=True)  50.4 us
    reduce_scatter x1, waiting for transfers between devices, per_device(): lax.psum_scatter(mlp_grads[4].astype(jnp.bfloat16), 'shard', scatter_dime...  40.4 us
    all_gather x1, waiting for transfers between devices, per_device(): lax.all_gather(up_weight, 'shard', axis=0, tiled=True)  23.3 us
    dot_general x1, matrix products, per_device(): jnp.einsum('nhqk,nkhe->nqhe', dscore, keys, preferred_element_type=single...  20.7 us
    dot_general x1, matrix products, per_device(): jnp.einsum('nhqk,nqhe->nkhe', dscore, query, preferred_element_type=singl...  19.3 us
  transfers between devices with their start and end apart: 8, of which 5 were waited for; matrix products, arithmetic and copies ran while one was open for 29% of the time, Pallas kernels for 0%

commit v1 on v0

--- a/solution.py
+++ b/solution.py
@@ -4,6 +4,28 @@
 from jax.sharding import PartitionSpec as P
 
 HEADS = 12
+
+
+def laid_out(parts, dim):
+    lengths = list(parts.shape[1:])
+    lengths[dim] *= parts.shape[0]
+    return jnp.moveaxis(parts, 0, dim).reshape(lengths)
+
+
+def doubled(x, axis):
+    count = lax.axis_size(axis)
+    blocks = x[None]
+    for level in range(count.bit_length() - 1):
+        apart = 1 << level
+        theirs = lax.ppermute(blocks, axis, [(i, i ^ apart) for i in range(count)])
+        both = jnp.stack([blocks, theirs])
+        upper = lax.axis_index(axis) >> level & 1
+        blocks = jnp.where(upper == 0, both, both[::-1]).reshape(-1, *x.shape)
+    return blocks
+
+
+def collect(x, axis, dim):
+    return laid_out(doubled(x, axis), dim)
 
 
 def matmul(left, right):
@@ -102,7 +124,7 @@
         lax.all_gather(second_norm_bias, "shard", axis=0, tiled=True),
         lax.all_gather(up_weight, "shard", axis=0, tiled=True),
         lax.all_gather(up_bias, "shard", axis=0, tiled=True),
-        lax.all_gather(down_weight, "shard", axis=0, tiled=True),
+        collect(down_weight, "shard", 0),
         lax.all_gather(down_bias, "shard", axis=0, tiled=True),
     )
     second_norm_gain = perceptron_complete[0].astype(single_float)

time: 832 us -> 873 us (1.049)
  blocking collectives: 345 us -> 427 us
  waiting for transfers between devices: 193 us -> 146 us
    all_gather x1, blocking collectives: 3.85 us -> 87.6 us  [per_device(): lax.all_gather(down_bias, 'shard', axis=0, tiled=True)]
    reduce_scatter x1, waiting for transfers between devices: 63 us -> 0.01 us  [per_device(): lax.psum_scatter(mlp_grads[2].astype(jnp.bfloat16), 'shard', scatter_dime...]
    reduce_scatter x1, waiting for transfers between devices: 40.4 us -> 55.9 us  [per_device(): lax.psum_scatter(mlp_grads[4].astype(jnp.bfloat16), 'shard', scatter_dime...]
  transfers between devices with their start and end apart: 8 -> 9, of which waited for: 5 -> 4; matrix products, arithmetic and copies ran while one was open for 29% -> 26% of each run, Pallas kernels for 0% -> 0%
where the time goes in v1:
time: 873 us; the launch traced here: 869 us
  blocking collectives  427 us (49%)
  matrix products  157 us (18%)
  waiting for transfers between devices  146 us (17%)
  local copies, waits for them, and re-layouts  102 us (12%)
  other arithmetic  20.1 us (2%)
  between operations  16.5 us (2%)
    psum x1, blocking collectives, per_device(): lax.psum((p_ln1_gain, p_ln1_bias, p_qkv, p_q_bias, p_v_bias, p_out, p_out...  305 us
    dot_general x12, matrix products, matmul(): return jnp.dot(left, right, preferred_element_type=jnp.float32)  92.3 us
    all_gather x1, blocking collectives, per_device(): lax.all_gather(down_bias, 'shard', axis=0, tiled=True)  87.6 us
    reduce_scatter x1, waiting for transfers between devices, per_device(): lax.psum_scatter(mlp_grads[4].astype(jnp.bfloat16), 'shard', scatter_dime...  55.9 us
    all_gather x1, waiting for transfers between devices, per_device(): lax.all_gather(down_weight, 'shard', axis=0, tiled=True)  50.6 us
    all_gather x1, waiting for transfers between devices, per_device(): lax.all_gather(up_weight, 'shard', axis=0, tiled=True)  23.4 us
    dot_general x1, matrix products, per_device(): jnp.einsum('nhqk,nkhe->nqhe', dscore, keys, preferred_element_type=single...  20.7 us
    dot_general x1, matrix products, per_device(): jnp.einsum('nhqk,nqhe->nkhe', dscore, query, preferred_element_type=singl...  19.4 us
  transfers between devices with their start and end apart: 9, of which 4 were waited for; matrix products, arithmetic and copies ran while one was open for 26% of the time, Pallas kernels for 0%

profile of v1, /device:TPU:1, one launch (start us, length us, event | category | flops | bytes accessed | tf_op | source)
XLA Modules:
  0.0 868.8 jit_solution(13663687220415570600)
XLA Ops:
  13.2 3.9 all-gather
  17.2 3.2 all-gather.1
  20.4 3.5 all-gather.2
  24.0 3.8 all-gather.3
  27.9 3.7 all-gather.4
  32.2 3.7 all-gather.5
  35.9 3.8 all-gather.7
  40.3 4.2 all-gather.6
  48.1 13.0 %all-gather.14.cloned.1.call-done = bf16[768,2304]{1,0:T(8,128)(2,1)} async-done(((bf16[384,2304]{1,0:T(8,128)(2,1)}), bf16[768,2304]{1,0:T(8,128)(2,1)}) %all-gather.14.cloned.1.call-update) | async-done | bytes 3538960 | tf_op jit(solution)/shard_map/all_gather | solution.py:84
  61.1 6.3 add_convert_fusion
  68.8 5.8 reshape.200
  74.6 6.0 copy.65
  80.6 4.4 reshape.201
  85.0 6.0 copy.66
  91.0 4.4 reshape.199
  95.4 5.4 copy.67
  100.8 4.1 multiply_reduce_fusion.1
  111.9 3.2 copy.69
  115.1 4.6 reshape.154
  119.8 4.4 fusion.45
  126.3 23.4 %all-gather.18.cloned.1.call-done = bf16[768,3072]{1,0:T(8,128)(2,1)} async-done(((bf16[384,3072]{1,0:T(8,128)(2,1)}), bf16[768,3072]{1,0:T(8,128)(2,1)}) %all-gather.18.cloned.1.call-update) | async-done | bytes 4718608 | tf_op jit(solution)/shard_map/all_gather | solution.py:125
  149.7 13.4 %multiply_convert_fusion.1 = (bf16[985,3072]{1,0:T(8,128)(2,1)}, f32[985,3072]{1,0:T(8,128)}) fusion(f32[3072]{0:T(1024)S(1)} %bitcast.53, bf16[768,3072]{1,0:T(8,128)(2,1)} %all-gather.18.cloned.1.call-done, f32[985,768]{1,0:T(8,128)} %copy-done.5, f32[768]{0:T(1024)S(1)} %copy-done.25, f32[768]{0:T(1024)S(1)} %reshape.186, f32[985]{0:T(1024)S(1)} %add_rsqrt_fusion.1, ...), kind=kOutput, calls=%fused_computation.12 | convolution fusion | flops 4669751296 | bytes 25926344 | tf_op jit(solution)/shard_map/dot_general | solution.py:32
  163.1 50.6 %all-gather.20.cloned.1.call-done = bf16[3072,768]{1,0:T(8,128)(2,1)} async-done(((bf16[1536,768]{1,0:T(8,128)(2,1)}), bf16[3072,768]{1,0:T(8,128)(2,1)}) %all-gather.20.cloned.1.call-update) | async-done | bytes 4718608 | tf_op jit(solution)/shard_map/all_gather | solution.py:150
  213.7 11.6 %fusion.48 = (bf16[3072]{0:T(1024)(128)(2,1)S(1)}, bf16[985,3072]{1,0:T(8,128)(2,1)S(1)}) fusion(f32[985,3072]{1,0:T(8,128)} %get-tuple-element.55, f32[3072]{0:T(1024)S(1)} %bitcast.54, bf16[985,768]{1,0:T(8,128)(2,1)S(1)} %copy-done.16, bf16[3072,768]{1,0:T(8,128)(2,1)} %all-gather.20.cloned.1.call-done), kind=kOutput, calls=%fused_computation.99 | convolution fusion | flops 4684121088 | bytes 24405504 | tf_op jit(solution)/shard_map/dot_general | solution.py:32
  225.3 5.5 multiply_reduce_fusion.3
  236.7 3.6 convolution_convert_fusion.3
  240.3 4.4 reshape.202
  244.6 6.1 copy.71
  250.7 10.0 %bitcast_convert_fusion = (bf16[5,197,12,64]{1,3,2,0:T(8,128)(2,1)}, f32[5,12,64,197]{3,2,1,0:T(8,128)}) fusion(bf16[5,197,12,64]{1,3,2,0:T(8,128)(2,1)} %copy.71, f32[5,12,197,197]{2,3,1,0:T(8,128)} %copy-done, f32[5,12,197]{2,1,0:T(8,128)S(1)} %copy-done.20), kind=kOutput, calls=%fused_computation.29 | convolution fusion | flops 305795232 | bytes 15413280 | tf_op jit(solution)/shard_map/nhqk,nqhe->nkhe/dot_general | solution.py:213
  260.8 8.0 fusion.49
  268.7 3.2 copy.81
  271.9 5.8 reshape.160
  277.7 19.4 %convert_bitcast_fusion = bf16[5,197,12,64]{1,3,2,0:T(8,128)(2,1)} fusion(bf16[5,197,12,64]{1,3,2,0:T(8,128)(2,1)S(1)} %copy-done.4, f32[5,12,197,197]{2,3,1,0:T(8,128)} %fusion.49, f32[5,12,197,197]{2,3,1,0:T(8,128)} %copy-done, f32[5,12,197]{2,1,0:T(8,128)S(1)} %copy-done.20), kind=kOutput, calls=%fused_computation.51 | convolution fusion | flops 319778464 | bytes 21701520 | tf_op jit(solution)/shard_map/nhqk,nqhe->nkhe/dot_general | solution.py:221
  297.2 4.7 copy.78
  301.8 5.7 reshape.159
  307.5 20.7 %bitcast_convert_fusion.1 = (bf16[5,197,12,64]{1,3,2,0:T(8,128)(2,1)}, f32[5,12,64,197]{3,2,1,0:T(8,128)}) fusion(bf16[5,197,12,64]{1,3,2,0:T(8,128)(2,1)S(1)} %copy-done.3, f32[5,12,197,197]{2,3,1,0:T(8,128)} %fusion.49, f32[5,12,197,197]{2,3,1,0:T(8,128)} %copy-done, f32[5,12,197]{2,1,0:T(8,128)S(1)} %copy-done.20), kind=kOutput, calls=%fused_computation.31 | convolution fusion | flops 319778464 | bytes 24727440 | tf_op jit(solution)/shard_map/nhqk,nkhe->nqhe/dot_general | solution.py:218
  328.2 3.0 copy.75
  331.2 3.5 reshape.158
  339.4 6.3 convolution_convert_fusion.2
  347.5 9.8 %convolution_convert_fusion.1 = bf16[768,3072]{1,0:T(8,128)(2,1)} fusion(bf16[985,3072]{1,0:T(8,128)(2,1)} %copy-done.37, f32[985,768]{1,0:T(8,128)S(1)} %copy-done.7, f32[768]{0:T(1024)S(1)} %copy-done.25, f32[768]{0:T(1024)S(1)} %reshape.186, f32[985]{0:T(1024)S(1)} %add_rsqrt_fusion.1, f32[985]{0:T(1024)S(1)} %broadcast_multiply_fusion.5), kind=kOutput, calls=%fused_computation.25 | convolution fusion | flops 4653955072 | bytes 13810376 | tf_op jit(solution)/shard_map/dot_general | solution.py:32
  357.3 9.1 %convolution_convert_fusion = bf16[3072,768]{1,0:T(8,128)(2,1)} fusion(bf16[985,3072]{1,0:T(8,128)(2,1)} %get-tuple-element.54, bf16[985,768]{1,0:T(8,128)(2,1)} %reshape.156), kind=kOutput, calls=%fused_computation.24 | convolution fusion | flops 4650172416 | bytes 12283392 | tf_op jit(solution)/shard_map/dot_general | solution.py:32
  370.4 87.6 %all-gather.8 = bf16[2,1,384]{2,1,0:T(2,128)(2,1)S(1)} all-gather(bf16[1,1,384]{2,1,0:T(2,128)(2,1)S(1)} %reshape.179), channel_id=1, replica_groups=mesh['rep'=16,'shard'=2] {'shard'}, dimensions={0}, use_global_device_ids=true | all-gather | bytes 2304 | tf_op jit(solution)/shard_map/all_gather | solution.py:128
  460.9 3.1 reverse_select_fusion
  466.8 9.8 %multiply_reduce_fusion.4 = (bf16[768]{0:T(1024)(128)(2,1)S(1)}, f32[985]{0:T(1024)S(1)}, f32[985]{0:T(1024)S(1)}, bf16[768]{0:T(1024)(128)(2,1)S(1)}, f32[985,768]{1,0:T(8,128)S(1)}) fusion(f32[985,768]{1,0:T(8,128)} %reshape.162, f32[985]{0:T(1024)S(1)} %rsqrt.20, f32[985]{0:T(1024)S(1)} %div.27, f32[768]{0:T(1024)S(1)} %reshape.181, ...), kind=kOutput, calls=%fused_computation.34 | convolution fusion | flops 3492664576 | bytes 14151568 | tf_op jit(solution)/shard_map/dot_general | solution.py:32
  481.9 10.1 %add_convert_fusion.2 = bf16[985,768]{1,0:T(8,128)(2,1)} fusion(f32[985,768]{1,0:T(8,128)S(1)} %copy-done.7, bf16[985,3072]{1,0:T(8,128)(2,1)} %get-tuple-element.54, bf16[3072,768]{1,0:T(8,128)(2,1)} %bitcast.52, f32[768]{0:T(1024)S(1)} %reshape.189), kind=kOutput, calls=%fused_computation.42 | convolution fusion | flops 4650083328 | bytes 15312384 | tf_op jit(solution)/shard_map/dot_general | solution.py:32
  494.9 5.2 all-reduce.10
  500.9 55.9 %reduce-scatter.11.cloned.1.call-done = bf16[1536,768]{1,0:T(8,128)(2,1)} async-done(((bf16[3072,768]{1,0:T(8,128)(2,1)}), bf16[1536,768]{1,0:T(8,128)(2,1)}) %reduce-scatter.11.cloned.1.call-update) | async-done | bytes 2359312 | tf_op jit(solution)/shard_map/reduce_scatter | solution.py:184
  556.8 304.7 %all-reduce.12 = (f32[384]{0:T(512)}, f32[384]{0:T(512)}, f32[384,2304]{1,0:T(8,128)}, f32[384]{0:T(512)}, f32[384]{0:T(512)}, /*index=5*/f32[384,768]{1,0:T(8,1...) all-reduce(f32[384]{0:T(512)S(1)} %dynamic-slice_convert_fusion.8, ...), channel_id=1, replica_groups=mesh['rep'=16,'shard'=2] {'rep'}, use_global_device_ids=true, to_apply=%region_13.14 | all-reduce | flops 3543552 | bytes 21270528 | tf_op jit(solution)/shard_map/psum | solution.py:287
  (168 shorter events, 51.0 us)
Async XLA Ops:
  7.2 53.9 %all-gather.14.cloned.1.call-start = ((), (), s32[]{:S(2)}) async-start(), calls=%async_computation.4 | async-start | bytes 5308416 | tf_op jit(solution)/shard_map/all_gather | solution.py:84
  7.9 2.2 copy-start.2
  7.9 111.8 %all-gather.16.cloned.1.call-start = ((), (), s32[]{:S(2)}) async-start(), calls=%async_computation.5 | async-start | bytes 1769472 | tf_op jit(solution)/shard_map/all_gather | solution.py:87
  8.7 141.0 %all-gather.18.cloned.1.call-start = ((), (), s32[]{:S(2)}) async-start(), calls=%async_computation.6 | async-start | bytes 7077888 | tf_op jit(solution)/shard_map/all_gather | solution.py:125
  9.4 204.3 %all-gather.20.cloned.1.call-start = ((), (), s32[]{:S(2)}) async-start(), calls=%async_computation.7 | async-start | bytes 7077888 | tf_op jit(solution)/shard_map/all_gather | solution.py:150
  10.0 3.2 copy-start.27
  10.0 7.1 copy-start.28
  10.0 10.4 %copy-start.29 = (bf16[384]{0:T(512)(128)(2,1)S(1)}, bf16[384]{0:T(512)(128)(2,1)}, u32[]{:S(2)}) copy-start(bf16[384]{0:T(512)(128)(2,1)} %param.19) | copy-start | bytes 2308
  10.0 14.0 %copy-start.30 = (bf16[384]{0:T(512)(128)(2,1)S(1)}, bf16[384]{0:T(512)(128)(2,1)}, u32[]{:S(2)}) copy-start(bf16[384]{0:T(512)(128)(2,1)} %param.20) | copy-start | bytes 2308
  10.0 17.9 %copy-start.31 = (bf16[384]{0:T(512)(128)(2,1)S(1)}, bf16[384]{0:T(512)(128)(2,1)}, u32[]{:S(2)}) copy-start(bf16[384]{0:T(512)(128)(2,1)} %param.22) | copy-start | bytes 2308
  10.0 22.2 %copy-start.32 = (bf16[384]{0:T(512)(128)(2,1)S(1)}, bf16[384]{0:T(512)(128)(2,1)}, u32[]{:S(2)}) copy-start(bf16[384]{0:T(512)(128)(2,1)} %param.23) | copy-start | bytes 2308
  10.0 25.9 %copy-start.26 = (bf16[1536]{0:T(1024)(128)(2,1)S(1)}, bf16[1536]{0:T(1024)(128)(2,1)}, u32[]{:S(2)}) copy-start(bf16[1536]{0:T(1024)(128)(2,1)} %param.26) | copy-start | bytes 9220
  10.1 30.3 %copy-start.33 = (bf16[384]{0:T(512)(128)(2,1)S(1)}, bf16[384]{0:T(512)(128)(2,1)}, u32[]{:S(2)}) copy-start(bf16[384]{0:T(512)(128)(2,1)} %param.24) | copy-start | bytes 2308
  10.1 490.8 %reduce-scatter.7.cloned.1.call-start = ((), (), s32[]{:S(2)}) async-start(), calls=%async_computation.9 | async-start | bytes 1769472 | tf_op jit(solution)/shard_map/reduce_scatter | solution.py:265
  13.0 48.1 %copy-start.10 = (f32[985,768]{1,0:T(8,128)S(1)}, f32[985,768]{1,0:T(8,128)}, u32[]{:S(2)}) copy-start(f32[985,768]{1,0:T(8,128)} %reshape.162) | copy-start | bytes 9077764
  20.4 47.0 %copy-start.23 = (f32[768]{0:T(1024)}, f32[768]{0:T(1024)S(1)}, u32[]{:S(2)}) copy-start(f32[768]{0:T(1024)S(1)} %reshape.182) | copy-start | bytes 9220
  104.9 4.5 copy-start
  109.4 2.5 copy-start.19
  119.7 4.4 copy-start.17
  124.2 1.6 copy-start.5
  124.2 25.5 %copy-start.22 = (f32[2,1,1536]{2,1,0:T(1,128)S(1)}, f32[2,1,1536]{2,1,0:T(1,128)}, u32[]{:S(2)}) copy-start(f32[2,1,1536]{2,1,0:T(1,128)} %convert_element_type.226) | copy-start | bytes 36868
  124.2 25.5 %copy-start.25 = (f32[768]{0:T(1024)S(1)}, f32[768]{0:T(1024)}, u32[]{:S(2)}) copy-start(f32[768]{0:T(1024)} %reshape.187) | copy-start | bytes 9220
  149.7 64.1 %copy-start.16 = (bf16[985,768]{1,0:T(8,128)(2,1)S(1)}, bf16[985,768]{1,0:T(8,128)(2,1)}, u32[]{:S(2)}) copy-start(bf16[985,768]{1,0:T(8,128)(2,1)} %reshape.156) | copy-start | bytes 4538884
  213.7 11.6 %copy-start.6 = (f32[985,768]{1,0:T(8,128)S(1)}, f32[985,768]{1,0:T(8,128)}, u32[]{:S(2)}) copy-start(f32[985,768]{1,0:T(8,128)} %copy-done.5) | copy-start | bytes 9077764
  213.7 11.6 %copy-start.35 = (bf16[768,3072]{1,0:T(8,128)(2,1)S(1)}, bf16[768,3072]{1,0:T(8,128)(2,1)}, u32[]{:S(2)}) copy-start(bf16[768,3072]{1,0:T(8,128)(2,1)} %all-gather.18.cloned.1.call-done) | copy-start | bytes 14155780
  225.3 5.5 copy-start.37
  230.9 3.4 copy-start.18
  232.6 1.7 copy-start.8
  244.6 6.1 copy-start.20
  260.7 240.1 %reduce-scatter.5.cloned.1.call-start = ((), (), s32[]{:S(2)}) async-start(), calls=%async_computation.8 | async-start | bytes 5308416 | tf_op jit(solution)/shard_map/reduce_scatter | solution.py:256
  260.8 8.0 copy-start.13
  271.9 5.8 copy-start.4
  301.8 5.7 copy-start.3
  334.7 1.9 copy-start.15
  334.7 2.4 copy-start.14
  336.6 2.8 copy-start.11
  336.6 2.8 copy-start.24
  337.2 2.2 copy-start.21
  345.6 1.9 copy-start.7
  345.6 155.2 %reduce-scatter.9.cloned.1.call-start = ((), (), s32[]{:S(2)}) async-start(), calls=%async_computation.10 | async-start | bytes 7077888 | tf_op jit(solution)/shard_map/reduce_scatter | solution.py:178
  357.3 199.5 %reduce-scatter.11.cloned.1.call-start = ((), (), s32[]{:S(2)}) async-start(), calls=%async_computation.11 | async-start | bytes 7077888 | tf_op jit(solution)/shard_map/reduce_scatter | solution.py:184
  366.5 2.0 copy-start.36
  366.5 3.9 copy-start.34
  366.5 91.5 %collective-permute-start = (bf16[1,1536,768]{2,1,0:T(8,128)(2,1)}, bf16[1,1536,768]{2,1,0:T(8,128)(2,1)}, u32[]{:S(2)}, u32[]{:S(2)}) collective-permute-start(bf16[1,1536,768]{2,1,0:T(8,128)(2,1)} %bitcast.50), channel_id=1, source_target_pairs={{0,1},{1,0},{2,3},{3,2},{4,5},{5,4},{6,7},{7,6},{8,9},{9,8},{10,11... | collective-permute-start | bytes 7077896 | tf_op jit(solution)/shard_map/ppermute | solution.py:20
  460.9 3.1 copy-start.1
  466.8 9.8 %copy-start.9 = (f32[985,768]{1,0:T(8,128)S(1)}, f32[985,768]{1,0:T(8,128)}, u32[]{:S(2)}) copy-start(f32[985,768]{1,0:T(8,128)} %copy-done.8) | copy-start | bytes 9077764
  466.8 9.8 %copy-start.12 = (f32[985,768]{1,0:T(8,128)S(1)}, f32[985,768]{1,0:T(8,128)}, u32[]{:S(2)}) copy-start(f32[985,768]{1,0:T(8,128)} %reshape.162) | copy-start | bytes 9077764
Sparse Core Ops, SparseCore 0:
  9.5 51.5 all-gather.13
  62.6 22.7 all-gather.15
  87.0 62.6 all-gather.17
  151.1 62.6 all-gather.19
  260.8 21.8 reduce-scatter.6
  345.8 69.4 reduce-scatter.4
  417.6 77.0 reduce-scatter.8
  496.9 59.7 reduce-scatter.10
